TPU v7x, 128 devices: a whole 4x4x4 slice. The times are simulated.
128 devices in a mesh: row: 16 (over z_lo, y, core), feat: 8 (over z_hi, x).
Axes of the slice: x: 4, y: 4, z: 4 (z_hi: 2, z_lo: 2; z = z_hi * 2 + z_lo), core: 2. Of those that a mesh axis runs over, the one named last changes fastest.
Arguments:
- features: bfloat16 [16384, 2048], P('row', 'feat'), may hold values from -6 to 6
- cut_points: float32 [2048, 256], P('feat'), as said below
- grad: float32 [16384], P('row'), may hold values from -1 to 1
- hess: float32 [16384], P('row'), may hold values from 0.05 to 0.25
- node_ids: int32 [16384], P('row'), may hold values from 0 to 31
Outputs:
- feature_gain: float32 [2048, 32], P(('feat', 'row'))
- node_best: float32 [32], replicated
Inputs may be any that keep to these rules, and one draw needn't show every extreme that they name: Each row of cut_points rises strictly.
All inputs are finite; a program needn't handle non-finite values.
Results may differ from a plain program's by a relative error of at most 0.0065.
Values may be sent and summed in bfloat16 or wider, within the bound.
No kernel may reach another device: no remote copies, remote signals or barrier semaphores. Data moves between devices by JAX's collectives and lax.ppermute only.
A program may use at most 128 MiB of HBM per device.

v0:
```python
import jax
import jax.numpy as jnp
from jax import lax
from jax.experimental import pallas as pl
from jax.experimental.pallas import tpu as pltpu
from jax.sharding import PartitionSpec as P

NODES = 32
PENALTY = 1.0
LANES = 128
COARSE = 8
FINE = 32
PIECE = 32
QUAD = 4
NODE_BLOCK = 4
PAIRED = 1


def dot_nt(left, right):
    return lax.dot_general(
        left, right, (((1,), (1,)), ((), ())), preferred_element_type=jnp.float32
    )


def iota(shape, axis):
    return lax.broadcasted_iota(jnp.int32, shape, axis)


def look_up(table, index):
    return jnp.take_along_axis(table, index, axis=1, mode="promise_in_bounds")


def sort_kernel(
    value_in, grad_in, hess_in, node_in, sent_ref, value_ref, grad_ref, hess_ref, node_ref, arrived
):
    pairs = ((node_in, node_ref), (grad_in, grad_ref), (hess_in, hess_ref), (value_in, value_ref))
    copies = [
        pltpu.make_async_copy(source, target, arrived.at[k])
        for k, (source, target) in enumerate(pairs)
    ]
    for copy in copies:
        copy.start()
    rows, feats = value_ref.shape
    parts = sent_ref.shape[0]
    own = feats // parts
    chunks = rows // LANES
    copies[0].wait()
    node = node_ref[...]
    member = (jnp.broadcast_to(node, (NODES, rows)) == iota((NODES, rows), 0)).astype(jnp.float32)
    earlier = (jnp.broadcast_to(node, (NODES, rows)) < iota((NODES, rows), 0)).astype(jnp.float32)
    upper = (iota((LANES, LANES), 0) <= iota((LANES, LANES), 1)).astype(jnp.bfloat16)
    offset = jnp.sum(earlier, axis=1, keepdims=True)
    ranks = []
    for c in range(chunks):
        piece = member[:, c * LANES : (c + 1) * LANES]
        running = jnp.dot(piece.astype(jnp.bfloat16), upper, preferred_element_type=jnp.float32)
        ranks.append(jnp.sum(piece * (running + (offset - 1.0)), axis=0, keepdims=True))
        offset = offset + jnp.sum(piece, axis=1, keepdims=True)
    rank = jnp.concatenate(ranks, axis=1).astype(jnp.int32)

    for copy in copies[1:]:
        copy.wait()
    side = jnp.concatenate(
        [grad_ref[...], hess_ref[...], node.astype(jnp.float32), jnp.zeros((13, rows), jnp.float32)],
        axis=0,
    ).astype(jnp.bfloat16)
    operand = jnp.concatenate([value_ref[...].T, side], axis=0)
    block = 2 * LANES
    sides = []
    for b in range(rows // block):
        chosen = jnp.where(
            jnp.broadcast_to(rank, (block, rows)) == iota((block, rows), 0) + b * block, 1.0, 0.0
        ).astype(jnp.bfloat16)
        moved = dot_nt(operand, chosen)
        for half in range(2):
            c = 2 * b + half
            lanes = slice(half * LANES, (half + 1) * LANES)
            sent_ref[:, c * own : (c + 1) * own, :] = (
                moved[:feats, lanes].astype(jnp.bfloat16).reshape(parts, own, LANES)
            )
            sides.append(moved[feats : feats + 3, lanes])
    packed = jnp.concatenate(
        [sides[c][i : i + 1] for i in range(3) for c in range(chunks)], axis=0
    ).astype(jnp.bfloat16)
    for d in range(parts):
        sent_ref[d, chunks * own :, :] = packed


def search_tables(edges):
    feats = edges.shape[0]
    lane = iota((feats, LANES), 1)
    low, high = edges[:, :LANES], edges[:, LANES:]

    def pick(index):
        place = jnp.where(index >= LANES, index - LANES, index)
        return jnp.where(
            index >= LANES,
            look_up(high, place),
            look_up(low, place),
        )

    inner = jnp.zeros((feats, LANES), jnp.int32)
    for level in range(7):
        start = 1 << level
        inner = jnp.where(lane >= start, (2 * (lane - start) + 1) * (1 << (7 - level)), inner)
    return pick(inner), pick(2 * lane + 1)


def gain_kernel(
    sent_ref, edge_ref, gain_ref, best_ref,
    side_ref, wide_edge_ref, even_fine_ref, even_coarse_ref, even_side_ref,
    odd_fine_ref, odd_coarse_ref, odd_side_ref,
    stat_ref, paired_ref, wide_ref, hist_ref, total_ref, top_ref,
):
    parts = sent_ref.shape[0]
    feats, bins = edge_ref.shape
    chunks = (sent_ref.shape[1] - 24) // feats
    per_vector = LANES // PIECE
    tile_rows = even_fine_ref.shape[2]
    quads = feats // QUAD

    hist_ref[...] = jnp.zeros_like(hist_ref)
    total = jnp.zeros((16, NODES), jnp.float32)
    for s in range(parts):
        side = sent_ref[s, chunks * feats :, :].astype(jnp.float32)
        side_ref[s] = side
        for c in range(0, chunks, 2):
            grad, hess, node = [
                jnp.concatenate([side[8 * i + c : 8 * i + c + 1], side[8 * i + c + 1 : 8 * i + c + 2]], axis=1)
                for i in range(3)
            ]
            wide = (NODES, 2 * LANES)
            member = jnp.where(
                jnp.broadcast_to(node, wide).astype(jnp.bfloat16)
                == iota(wide, 0).astype(jnp.float32).astype(jnp.bfloat16),
                jnp.bfloat16(1),
                jnp.bfloat16(0),
            )
            both = jnp.concatenate(
                [jnp.broadcast_to(grad, (8, 2 * LANES)), jnp.broadcast_to(hess, (8, 2 * LANES))], axis=0
            ).astype(jnp.bfloat16)
            total = total + dot_nt(both, member)
    spread = jnp.concatenate([total, jnp.zeros((16, LANES - NODES), jnp.float32)], axis=1)
    for n in range(NODES):
        total_ref[n] = jnp.broadcast_to(spread[:, n : n + 1], (16, LANES))

    edges = edge_ref[...]
    inner, leaf = search_tables(edges)

    for j in range(8):
        wide_edge_ref[j] = jnp.broadcast_to(edges[:, 32 * j : 32 * j + 1], (feats, LANES))

    def search(value):
        bits = []
        for level in range(3):
            choice = [wide_edge_ref[(2 * m + 1) << (2 - level)] for m in range(1 << level)]
            for bit in reversed(bits):
                choice = [
                    jnp.where(bit, choice[2 * m + 1], choice[2 * m])
                    for m in range(len(choice) // 2)
                ]
            bits.append(value >= choice[0])
        place = jnp.where(bits[0], 12, 8)
        for level in range(1, 3):
            place = place + jnp.where(bits[level], 4 >> level, 0)
        for level in range(3, 8):
            if level < 7:
                edge = look_up(inner, place)
            else:
                edge = look_up(leaf, place - LANES)
            place = place + place + jnp.where(value >= edge, 1, 0)
        return jnp.where(value >= wide_edge_ref[0], place - 256, -1)

    def shuffle(pieces, block):
        pieces = list(pieces)
        step = per_vector // 2
        while step >= 1:
            keep = (block & step) == 0
            for s in range(per_vector):
                if s & step == 0:
                    a, b = pieces[s], pieces[s + step]
                    pieces[s] = jnp.where(keep, a, pltpu.roll(b, step * PIECE, 1))
                    pieces[s + step] = jnp.where(keep, pltpu.roll(a, LANES - step * PIECE, 1), b)
            step //= 2
        return pieces

    block = iota((feats, LANES), 1) // PIECE
    block_side = iota((3, LANES), 1) // PIECE

    def prepare(c, fine_ref, coarse_ref, side_tile_ref):
        least, most = [None] * per_vector, [None] * per_vector
        for q in range(parts // per_vector):
            slots, sides = [], []
            for s in range(q * per_vector, (q + 1) * per_vector):
                value = sent_ref[s, pl.ds(pl.multiple_of(c * feats, feats), feats), :]
                slots.append(search(value.astype(jnp.float32)))
                sides.append(side_ref[s, pl.ds(c, 3, stride=8), :])
            lanes = slice(q * LANES, (q + 1) * LANES)
            for j, slot in enumerate(shuffle(slots, block)):
                coarse_ref[j, :, lanes] = (slot >> 5).astype(jnp.float32)
                fine_ref[j, :, lanes] = (slot & 31).astype(jnp.float32)
            for j, side in enumerate(shuffle(sides, block_side)):
                side_tile_ref[j, 0:3, lanes] = side
                node = side[2:3]
                least[j] = node if q == 0 else jnp.minimum(least[j], node)
                most[j] = node if q == 0 else jnp.maximum(most[j], node)
        return [
            (
                jnp.minimum(jnp.min(least[j]).astype(jnp.int32), NODES - NODE_BLOCK),
                jnp.max(most[j]).astype(jnp.int32),
            )
            for j in range(per_vector)
        ]

    deep = 2 * COARSE
    pair_rows = (deep, tile_rows)
    step_index = (iota(pair_rows, 0) & 7).astype(jnp.float32)
    fine_index = [(step_index + 8.0 * j).astype(jnp.bfloat16) for j in range(FINE // 8)]
    coarse_index = step_index.astype(jnp.bfloat16)
    quarter_lane = iota((COARSE, LANES), 1)
    quarter = ((quarter_lane >> 6) << 1) | ((quarter_lane >> 3) & 1)
    zero = jnp.bfloat16(0)
    one = jnp.bfloat16(1)
    two = jnp.bfloat16(2)

    def mask_nodes(first, count, node_wide, both):
        return [
            jnp.where(node_wide == (first + b).astype(jnp.float32).astype(jnp.bfloat16), part, zero)
            for b in range(count)
            for part in both
        ]

    def add_product(u, q, first, masked):
        here = [wide_ref[u, q * (QUAD // 2) + i] for i in range(QUAD // 2)]
        stream = jnp.concatenate([h * m for m in masked for h in here], axis=0)
        product = dot_nt(stream, stat_ref[u, q])
        for k in range(len(masked)):
            add_block(first + k // 2, q, k % 2, product[k * 32 : k * 32 + 32])

    def add_block(n, q, k, part):
        packed = part[:COARSE]
        for i in range(1, QUAD):
            packed = jnp.where(quarter == i, part[COARSE * i : COARSE * (i + 1)], packed)
        hist_ref[n, q, k * COARSE : (k + 1) * COARSE] += packed

    def add_paired(u, q, first, masked):
        here = [wide_ref[u, q * (QUAD // 2) + i] for i in range(QUAD // 2)]
        stream = jnp.concatenate([h * m for m in masked for h in here], axis=0)
        product = dot_nt(stream, paired_ref[u, q - (quads - PAIRED)])
        for k in range(len(masked)):
            for odd in range(2):
                add_block(
                    first + 2 * (k // 2) + odd, q, k % 2,
                    product[k * 32 : k * 32 + 32, odd * LANES : (odd + 1) * LANES],
                )

    def tile_sides(side_tile_ref, u):
        grad, hess, node = [
            jnp.broadcast_to(side_tile_ref[u, k : k + 1, :], pair_rows).astype(jnp.bfloat16)
            for k in range(3)
        ]
        return node, (grad, hess)

    def pair_of(ref, u, f):
        return jnp.concatenate(
            [
                jnp.broadcast_to(ref[u, f + k : f + k + 1, :], (COARSE, tile_rows))
                for k in range(2)
            ],
            axis=0,
        ).astype(jnp.bfloat16)

    def accumulate(ranges, fine_ref, coarse_ref, side_tile_ref):
        for u in range(per_vector):
            node_wide, both = tile_sides(side_tile_ref, u)
            first = ranges[u][0]
            masked = mask_nodes(first, NODE_BLOCK, node_wide, both)
            place = node_wide - first.astype(jnp.float32).astype(jnp.bfloat16)
            second = place >= two
            coupled = [jnp.where(second, zero, part) for part in both] + [
                jnp.where(second, part, zero) for part in both
            ]
            parity = [
                jnp.where(place == jnp.bfloat16(k), one, jnp.where(place == jnp.bfloat16(k + 2), one, zero))
                for k in range(2)
            ]
            for q in range(quads):
                for i in range(QUAD // 2):
                    f = q * QUAD + 2 * i
                    fine = pair_of(fine_ref, u, f)
                    for j in range(FINE // 8):
                        at = i * 2 * FINE + deep * j
                        inside = fine <= fine_index[j]
                        if q < quads - PAIRED:
                            stat_ref[u, q, at : at + deep, :] = jnp.where(inside, one, zero)
                        else:
                            for k in range(2):
                                low = k * LANES + at
                                paired_ref[u, q - (quads - PAIRED), low : low + deep, :] = (
                                    jnp.where(inside, parity[k], zero)
                                )
                    coarse = pair_of(coarse_ref, u, f)
                    wide_ref[u, f // 2] = jnp.where(coarse == coarse_index, one, zero)
                if q < quads - PAIRED:
                    add_product(u, q, first, masked)
                else:
                    add_paired(u, q, first, coupled)

    def accumulate_rest(ranges, fine_ref, side_tile_ref):
        for u in range(per_vector):
            first, last = ranges[u]

            @pl.loop(first + NODE_BLOCK, last + 1)
            def _(n):
                node_wide, both = tile_sides(side_tile_ref, u)
                masked = mask_nodes(n, 1, node_wide, both)
                for q in range(quads):
                    if q >= quads - PAIRED:
                        for i in range(QUAD // 2):
                            fine = pair_of(fine_ref, u, q * QUAD + 2 * i)
                            for j in range(FINE // 8):
                                at = i * 2 * FINE + deep * j
                                stat_ref[u, q, at : at + deep, :] = jnp.where(
                                    fine <= fine_index[j], one, zero
                                )
                    add_product(u, q, n, masked)

    even = (even_fine_ref, even_coarse_ref, even_side_ref)
    odd = (odd_fine_ref, odd_coarse_ref, odd_side_ref)

    def two_chunks(pair, ranges):
        accumulate(ranges, *even)
        later = prepare(2 * pair + 1, *odd)
        accumulate_rest(ranges, even_fine_ref, even_side_ref)
        accumulate(later, *odd)
        following = prepare(jnp.minimum(2 * pair + 2, chunks - 1), *even)
        accumulate_rest(later, odd_fine_ref, odd_side_ref)
        return following

    lax.fori_loop(0, chunks // 2, two_chunks, prepare(0, *even))

    row = iota((COARSE, LANES), 0)
    last_lane = iota((COARSE, LANES), 1) | 55

    def left_sums(part):
        ends = look_up(part, last_lane)
        shift = 1
        while shift < COARSE:
            ends = ends + jnp.where(row >= shift, pltpu.roll(ends, shift, 0), 0.0)
            shift *= 2
        return part + jnp.where(row >= 1, pltpu.roll(ends, 1, 0), 0.0)

    @pl.loop(0, NODES // 4)
    def _(group):
        for k in range(4):
            n = 4 * group + k
            grad_total = total_ref[n, :COARSE]
            hess_total = total_ref[n, COARSE:]
            whole = jnp.square(grad_total) / (hess_total + PENALTY)
            for q in range(quads):
                part = hist_ref[n, q]
                grad_left = left_sums(part[:COARSE])
                hess_left = left_sums(part[COARSE:])
                split = jnp.square(grad_left) / (hess_left + PENALTY)
                split = split + jnp.square(grad_total - grad_left) / (
                    hess_total - hess_left + PENALTY
                )
                split = split - whole
                top_ref[q, pl.ds(n, 1), :] = jnp.max(split, axis=0, keepdims=True)

    best = None
    for q in range(quads):
        top = top_ref[q]
        for shift in (32, 16, 4, 2, 1):
            top = jnp.maximum(top, pltpu.roll(top, LANES - shift, 1))
        turned = top.T
        for i in range(QUAD):
            found = turned[64 * (i // 2) + 8 * (i % 2) : 64 * (i // 2) + 8 * (i % 2) + 1]
            gain_ref[QUAD * q + i : QUAD * q + i + 1] = found
            best = found if best is None else jnp.maximum(best, found)
    best_ref[...] = jnp.broadcast_to(best, best_ref.shape)


def on_device(features, cut_points, grad, hess, node_ids):
    parts = lax.axis_size("row")
    others = parts * lax.axis_size("feat")
    rows, feats = features.shape
    own = feats // parts
    bins = cut_points.shape[1]
    length = (own + 3) * rows // LANES
    in_vmem = pl.BlockSpec(memory_space=pltpu.VMEM)
    sent = pl.pallas_call(
        sort_kernel,
        out_shape=jax.ShapeDtypeStruct((parts, length, LANES), jnp.bfloat16),
        in_specs=[pl.BlockSpec(memory_space=pltpu.MemorySpace.HBM)] * 4,
        out_specs=in_vmem,
        scratch_shapes=[
            pltpu.VMEM((rows, feats), jnp.bfloat16),
            pltpu.VMEM((1, rows), jnp.float32),
            pltpu.VMEM((1, rows), jnp.float32),
            pltpu.VMEM((1, rows), jnp.int32),
            pltpu.SemaphoreType.DMA((4,)),
        ],
        name="sort_rows",
        compiler_params=pltpu.CompilerParams(vmem_limit_bytes=67043328),
    )(features, grad[None], hess[None], node_ids[None])
    gathered = lax.all_to_all(sent, "row", 0, 0)
    edges = lax.dynamic_slice_in_dim(cut_points, lax.axis_index("row") * own, own, 0)
    tile_rows = PIECE * parts
    feature_gain, best = pl.pallas_call(
        gain_kernel,
        out_shape=(
            jax.ShapeDtypeStruct((own, NODES), jnp.float32),
            jax.ShapeDtypeStruct((others, NODES), jnp.float32),
        ),
        in_specs=[in_vmem] * 2,
        out_specs=(in_vmem, in_vmem),
        scratch_shapes=[
            pltpu.VMEM((parts, 24, LANES), jnp.float32),
            pltpu.VMEM((8, own, LANES), jnp.float32),
            *[
                pltpu.VMEM((LANES // PIECE, height, tile_rows), jnp.float32)
                for height in (own, own, 8, own, own, 8)
            ],
            pltpu.VMEM((LANES // PIECE, own // QUAD, QUAD * FINE, tile_rows), jnp.bfloat16),
            pltpu.VMEM((LANES // PIECE, PAIRED, 2 * QUAD * FINE, tile_rows), jnp.bfloat16),
            pltpu.VMEM((LANES // PIECE, own // 2, 2 * COARSE, tile_rows), jnp.bfloat16),
            pltpu.VMEM((NODES, own // QUAD, 2 * COARSE, LANES), jnp.float32),
            pltpu.VMEM((NODES, 2 * COARSE, LANES), jnp.float32),
            pltpu.VMEM((own // QUAD, NODES, LANES), jnp.float32),
        ],
        name="split_gain",
        compiler_params=pltpu.CompilerParams(vmem_limit_bytes=40 << 20),
    )(gathered, edges)
    node_best = jnp.max(lax.all_to_all(best, ("row", "feat"), 0, 0), axis=0)
    return (feature_gain, node_best)


def solution(mesh):
    placed = (P("row", "feat"), P("feat", None), P("row"), P("row"), P("row"))
    return jax.shard_map(
        on_device,
        mesh=mesh,
        in_specs=placed,
        out_specs=(P(("feat", "row"), None), P()),
        check_vma=False,
    )
```

profile of v0, /device:TPU:1, one launch (start us, length us, event | category | flops | bytes accessed | tf_op | source)
XLA Modules:
  0.0 53.7 jit_solution(9878214961218634650)
XLA Ops:
  0.6 2.7 %sort_rows.1 = bf16[16,152,128]{2,1,0:T(8,128)(2,1)} custom-call(bf16[1024,256]{1,0:T(8,128)(2,1)} %value_in.1, f32[1,1024]{1,0:T(1,128)} %bitcast.7, f32[1,1024]{1,0:T(1,128)} %bitcast.8, s32[1,1024]{1,0:T(1,128)} %bitcast.9), custom_call_target="tpu_custom_call" | custom-call | tf_op jit(solution)/shard_map/sort_rows/pallas_call | solution.py:392
  3.4 7.4 %all-to-all-start = ((bf16[16,152,128]{2,1,0:T(8,128)(2,1)}), bf16[16,152,128]{2,1,0:T(8,128)(2,1)S(1)}, u32[]{:S(2)}, u32[]{:S(2)}) async-start(bf16[16,152,128]{2,1,0:T(8,128)(2,1)} %sort_rows.1), calls=%async_computation | async-start | bytes 1245184 | tf_op jit(solution)/shard_map/all_to_all | solution.py:407
  10.7 0.7 %constant_dynamic-slice_fusion.edge_ref = f32[16,256]{1,0:T(8,128)S(1)} fusion(f32[256,256]{1,0:T(8,128)} %param.6, s32[]{:T(128)S(6)} %select_n.3), kind=kLoop, calls=%fused_computation | loop fusion | bytes 32772 | tf_op jit(solution)/shard_map/dynamic_slice | solution.py:408
  11.4 10.3 %all-to-all-done.sent_ref = bf16[16,152,128]{2,1,0:T(8,128)(2,1)S(1)} async-done(((bf16[16,152,128]{2,1,0:T(8,128)(2,1)}), bf16[16,152,128]{2,1,0:T(8,128)(2,1)S(1)}, u32[]{:S(2)}, u32[]{:S(2)}) %all-to-all-start) | async-done | bytes 622624 | tf_op jit(solution)/shard_map/all_to_all | solution.py:407
  21.7 14.3 %split_gain.1 = (f32[16,32]{1,0:T(8,128)}, f32[128,32]{1,0:T(8,128)S(1)}) custom-call(bf16[16,152,128]{2,1,0:T(8,128)(2,1)S(1)} %all-to-all-done.sent_ref, f32[16,256]{1,0:T(8,128)S(1)} %constant_dynamic-slice_fusion.edge_ref), custom_call_target="tpu_custom_call" | custom-call | tf_op jit(solution)/shard_map/split_gain/pallas_call | solution.py:410
  36.0 17.0 %all_to_all.14 = f32[128,1,32]{2,1,0:T(1,128)S(1)} all-to-all(f32[128,1,32]{2,1,0:T(1,128)S(1)} %bitcast.6), channel_id=1, replica_groups=mesh['row'=16,'feat'=8] {'row','feat'}, dimensions={0} | all-to-all | bytes 32768 | tf_op jit(solution)/shard_map/all_to_all | solution.py:435
  53.1 0.7 %reduce_max.9 = f32[32]{0:T(128)} reduce(f32[128,1,32]{2,1,0:T(1,128)S(1)} %all_to_all.14, f32[]{:T(128)} %constant.13.clone.1), dimensions={0,1}, to_apply=%region_0.0 | reduce | flops 4064 | bytes 16516 | tf_op jit(solution)/shard_map/reduce_max | solution.py:435
Async XLA Ops:
  3.4 18.4 %all-to-all-start = ((bf16[16,152,128]{2,1,0:T(8,128)(2,1)}), bf16[16,152,128]{2,1,0:T(8,128)(2,1)S(1)}, u32[]{:S(2)}, u32[]{:S(2)}) async-start(bf16[16,152,128]{2,1,0:T(8,128)(2,1)} %sort_rows.1), calls=%async_computation | async-start | bytes 1245184 | tf_op jit(solution)/shard_map/all_to_all | solution.py:407
where the time goes:
time: 54 us; the launch traced here: 53.7 us
  Pallas kernels  17 us (31%)
  blocking collectives  17 us (31%)
  waiting for transfers between devices  10.3 us (19%)
  starting transfers between devices  7.35 us (14%)
  local copies, waits for them, and re-layouts  0.72 us (1%)
  other arithmetic  0.66 us (1%)
  between operations  0.64 us (1%)
    all_to_all x1, blocking collectives, on_device(): node_best = jnp.max(lax.all_to_all(best, ('row', 'feat'), 0, 0), axis=0)  17 us
    pallas_call x1, Pallas kernels, on_device(): pl.pallas_call(gain_kernel, out_shape=(jax.ShapeDtypeStruct((own, NODES),...  14.3 us
    all_to_all x1, waiting for transfers between devices, on_device(): gathered = lax.all_to_all(sent, 'row', 0, 0)  10.3 us
    all_to_all x1, starting transfers between devices, on_device(): gathered = lax.all_to_all(sent, 'row', 0, 0)  7.35 us
    pallas_call x1, Pallas kernels, on_device(): pl.pallas_call(sort_kernel, out_shape=jax.ShapeDtypeStruct((parts, length...  2.73 us
  transfers between devices with their start and end apart: 1, of which 1 were waited for; matrix products, arithmetic and copies ran while one was open for 1% of the time, Pallas kernels for 0%

commit v1 on v0

--- a/solution.py
+++ b/solution.py
@@ -379,6 +379,11 @@
             gain_ref[QUAD * q + i : QUAD * q + i + 1] = found
             best = found if best is None else jnp.maximum(best, found)
     best_ref[...] = jnp.broadcast_to(best, best_ref.shape)
+
+
+def finish_kernel(own_ref, all_ref, gain_ref, best_ref):
+    gain_ref[...] = own_ref[...]
+    best_ref[...] = jnp.max(all_ref[...], axis=0, keepdims=True)
 
 
 def on_device(features, cut_points, grad, hess, node_ids):
@@ -432,8 +437,18 @@
         name="split_gain",
         compiler_params=pltpu.CompilerParams(vmem_limit_bytes=40 << 20),
     )(gathered, edges)
-    node_best = jnp.max(lax.all_to_all(best, ("row", "feat"), 0, 0), axis=0)
-    return (feature_gain, node_best)
+    feature_gain, node_best = pl.pallas_call(
+        finish_kernel,
+        out_shape=(
+            jax.ShapeDtypeStruct((own, NODES), jnp.float32),
+            jax.ShapeDtypeStruct((1, NODES), jnp.float32),
+        ),
+        in_specs=[in_vmem] * 2,
+        out_specs=(in_vmem, in_vmem),
+        name="write_gains",
+        compiler_params=pltpu.CompilerParams(vmem_limit_bytes=4 << 20),
+    )(feature_gain, lax.all_to_all(best, ("row", "feat"), 0, 0))
+    return (feature_gain, node_best[0])
 
 
 def solution(mesh):

time: 54 us -> 53.6 us (level)
  other arithmetic: 0.66 us -> 0 us
    reduce_max x1 -> x0, other arithmetic: 0.66 us -> none  [on_device(): node_best = jnp.max(lax.all_to_all(best, ('row', 'feat'), 0, 0), axis=0)]
    pallas_call x0 -> x1, Pallas kernels: none -> 0.6 us  [on_device(): pl.pallas_call(finish_kernel, out_shape=(jax.ShapeDtypeStruct((own, NODES...]
    pallas_call x1, Pallas kernels: 14.3 us -> 13.7 us  [on_device(): pl.pallas_call(gain_kernel, out_shape=(jax.ShapeDtypeStruct((own, NODES),...]
where the time goes in v1:
time: 53.6 us; the launch traced here: 53.1 us
  Pallas kernels  17.1 us (32%)
  blocking collectives  17 us (32%)
  waiting for transfers between devices  10.3 us (19%)
  starting transfers between devices  7.35 us (14%)
  local copies, waits for them, and re-layouts  0.72 us (1%)
  between operations  0.65 us (1%)
    all_to_all x1, blocking collectives, on_device(): lax.all_to_all(best, ('row', 'feat'), 0, 0)  17 us
    pallas_call x1, Pallas kernels, on_device(): pl.pallas_call(gain_kernel, out_shape=(jax.ShapeDtypeStruct((own, NODES),...  13.7 us
    all_to_all x1, waiting for transfers between devices, on_device(): gathered = lax.all_to_all(sent, 'row', 0, 0)  10.3 us
    all_to_all x1, starting transfers between devices, on_device(): gathered = lax.all_to_all(sent, 'row', 0, 0)  7.35 us
    pallas_call x1, Pallas kernels, on_device(): pl.pallas_call(sort_kernel, out_shape=jax.ShapeDtypeStruct((parts, length...  2.74 us
  transfers between devices with their start and end apart: 1, of which 1 were waited for; matrix products, arithmetic and copies ran while one was open for 1% of the time, Pallas kernels for 0%

profile of v1, /device:TPU:1, one launch (start us, length us, event | category | flops | bytes accessed | tf_op | source)
XLA Modules:
  0.0 53.1 jit_solution(2701369983581302596)
XLA Ops:
  0.6 2.7 %sort_rows.1 = bf16[16,152,128]{2,1,0:T(8,128)(2,1)} custom-call(bf16[1024,256]{1,0:T(8,128)(2,1)} %value_in.1, f32[1,1024]{1,0:T(1,128)} %bitcast.10, f32[1,1024]{1,0:T(1,128)} %bitcast.11, s32[1,1024]{1,0:T(1,128)} %bitcast.12), custom_call_target="tpu_custom_call" | custom-call | tf_op jit(solution)/shard_map/sort_rows/pallas_call | solution.py:397
  3.4 7.4 %all-to-all-start = ((bf16[16,152,128]{2,1,0:T(8,128)(2,1)}), bf16[16,152,128]{2,1,0:T(8,128)(2,1)S(1)}, u32[]{:S(2)}, u32[]{:S(2)}) async-start(bf16[16,152,128]{2,1,0:T(8,128)(2,1)} %sort_rows.1), calls=%async_computation | async-start | bytes 1245184 | tf_op jit(solution)/shard_map/all_to_all | solution.py:412
  10.7 0.7 %constant_dynamic-slice_fusion.edge_ref = f32[16,256]{1,0:T(8,128)S(1)} fusion(f32[256,256]{1,0:T(8,128)} %param.6, s32[]{:T(128)S(6)} %select_n.3), kind=kLoop, calls=%fused_computation | loop fusion | bytes 32772 | tf_op jit(solution)/shard_map/dynamic_slice | solution.py:413
  11.5 10.3 %all-to-all-done.sent_ref = bf16[16,152,128]{2,1,0:T(8,128)(2,1)S(1)} async-done(((bf16[16,152,128]{2,1,0:T(8,128)(2,1)}), bf16[16,152,128]{2,1,0:T(8,128)(2,1)S(1)}, u32[]{:S(2)}, u32[]{:S(2)}) %all-to-all-start) | async-done | bytes 622624 | tf_op jit(solution)/shard_map/all_to_all | solution.py:412
  21.8 13.7 %split_gain.1 = (f32[16,32]{1,0:T(8,128)S(1)}, f32[128,32]{1,0:T(8,128)S(1)}) custom-call(bf16[16,152,128]{2,1,0:T(8,128)(2,1)S(1)} %all-to-all-done.sent_ref, f32[16,256]{1,0:T(8,128)S(1)} %constant_dynamic-slice_fusion.edge_ref), custom_call_target="tpu_custom_call" | custom-call | tf_op jit(solution)/shard_map/split_gain/pallas_call | solution.py:415
  35.5 17.0 %all_to_all.16 = f32[128,1,32]{2,1,0:T(1,128)S(1)} all-to-all(f32[128,1,32]{2,1,0:T(1,128)S(1)} %bitcast.9), channel_id=1, replica_groups=mesh['row'=16,'feat'=8] {'row','feat'}, dimensions={0} | all-to-all | bytes 32768 | tf_op jit(solution)/shard_map/all_to_all | solution.py:450
  52.5 0.6 %write_gains.1 = (f32[16,32]{1,0:T(8,128)}, f32[1,32]{1,0:T(1,128)}) custom-call(f32[16,32]{1,0:T(8,128)S(1)} %get-tuple-element.6.own_ref, f32[128,32]{1,0:T(8,128)S(1)} %bitcast.8), custom_call_target="tpu_custom_call" | custom-call | tf_op jit(solution)/shard_map/write_gains/pallas_call | solution.py:440
Async XLA Ops:
  3.4 18.4 %all-to-all-start = ((bf16[16,152,128]{2,1,0:T(8,128)(2,1)}), bf16[16,152,128]{2,1,0:T(8,128)(2,1)S(1)}, u32[]{:S(2)}, u32[]{:S(2)}) async-start(bf16[16,152,128]{2,1,0:T(8,128)(2,1)} %sort_rows.1), calls=%async_computation | async-start | bytes 1245184 | tf_op jit(solution)/shard_map/all_to_all | solution.py:412

commit v2 on v1

--- a/solution.py
+++ b/solution.py
@@ -13,7 +13,7 @@
 PIECE = 32
 QUAD = 4
 NODE_BLOCK = 4
-PAIRED = 1
+PAIRED = (0, 2)
 
 
 def dot_nt(left, right):
@@ -246,7 +246,7 @@
     def add_paired(u, q, first, masked):
         here = [wide_ref[u, q * (QUAD // 2) + i] for i in range(QUAD // 2)]
         stream = jnp.concatenate([h * m for m in masked for h in here], axis=0)
-        product = dot_nt(stream, paired_ref[u, q - (quads - PAIRED)])
+        product = dot_nt(stream, paired_ref[u, PAIRED.index(q)])
         for k in range(len(masked)):
             for odd in range(2):
                 add_block(
@@ -291,39 +291,46 @@
                     for j in range(FINE // 8):
                         at = i * 2 * FINE + deep * j
                         inside = fine <= fine_index[j]
-                        if q < quads - PAIRED:
+                        if q not in PAIRED:
                             stat_ref[u, q, at : at + deep, :] = jnp.where(inside, one, zero)
                         else:
                             for k in range(2):
                                 low = k * LANES + at
-                                paired_ref[u, q - (quads - PAIRED), low : low + deep, :] = (
+                                paired_ref[u, PAIRED.index(q), low : low + deep, :] = (
                                     jnp.where(inside, parity[k], zero)
                                 )
                     coarse = pair_of(coarse_ref, u, f)
                     wide_ref[u, f // 2] = jnp.where(coarse == coarse_index, one, zero)
-                if q < quads - PAIRED:
+                if q not in PAIRED:
                     add_product(u, q, first, masked)
                 else:
                     add_paired(u, q, first, coupled)
 
     def accumulate_rest(ranges, fine_ref, side_tile_ref):
-        for u in range(per_vector):
-            first, last = ranges[u]
-
-            @pl.loop(first + NODE_BLOCK, last + 1)
-            def _(n):
-                node_wide, both = tile_sides(side_tile_ref, u)
-                masked = mask_nodes(n, 1, node_wide, both)
-                for q in range(quads):
-                    if q >= quads - PAIRED:
-                        for i in range(QUAD // 2):
-                            fine = pair_of(fine_ref, u, q * QUAD + 2 * i)
-                            for j in range(FINE // 8):
-                                at = i * 2 * FINE + deep * j
-                                stat_ref[u, q, at : at + deep, :] = jnp.where(
-                                    fine <= fine_index[j], one, zero
-                                )
-                    add_product(u, q, n, masked)
+        most = ranges[0][1] - ranges[0][0]
+        for first, last in ranges[1:]:
+            most = jnp.maximum(most, last - first)
+
+        @pl.when(most >= NODE_BLOCK)
+        def _():
+            for u in range(per_vector):
+                tile_rest(u, *ranges[u], fine_ref, side_tile_ref)
+
+    def tile_rest(u, first, last, fine_ref, side_tile_ref):
+        @pl.loop(first + NODE_BLOCK, last + 1)
+        def _(n):
+            node_wide, both = tile_sides(side_tile_ref, u)
+            masked = mask_nodes(n, 1, node_wide, both)
+            for q in range(quads):
+                if q in PAIRED:
+                    for i in range(QUAD // 2):
+                        fine = pair_of(fine_ref, u, q * QUAD + 2 * i)
+                        for j in range(FINE // 8):
+                            at = i * 2 * FINE + deep * j
+                            stat_ref[u, q, at : at + deep, :] = jnp.where(
+                                fine <= fine_index[j], one, zero
+                            )
+                add_product(u, q, n, masked)
 
     even = (even_fine_ref, even_coarse_ref, even_side_ref)
     odd = (odd_fine_ref, odd_coarse_ref, odd_side_ref)
@@ -428,7 +435,7 @@
                 for height in (own, own, 8, own, own, 8)
             ],
             pltpu.VMEM((LANES // PIECE, own // QUAD, QUAD * FINE, tile_rows), jnp.bfloat16),
-            pltpu.VMEM((LANES // PIECE, PAIRED, 2 * QUAD * FINE, tile_rows), jnp.bfloat16),
+            pltpu.VMEM((LANES // PIECE, len(PAIRED), 2 * QUAD * FINE, tile_rows), jnp.bfloat16),
             pltpu.VMEM((LANES // PIECE, own // 2, 2 * COARSE, tile_rows), jnp.bfloat16),
             pltpu.VMEM((NODES, own // QUAD, 2 * COARSE, LANES), jnp.float32),
             pltpu.VMEM((NODES, 2 * COARSE, LANES), jnp.float32),

time: 53.6 us -> 53.2 us (level)
  no operation moved by 1% of the time
where the time goes in v2:
time: 53.2 us
  Pallas kernels  17.2 us (32%)
  blocking collectives  17 us (32%)
  waiting for transfers between devices  10.3 us (19%)
  starting transfers between devices  7.35 us (14%)
  local copies, waits for them, and re-layouts  0.72 us (1%)
  between operations  0.65 us (1%)
    all_to_all x1, blocking collectives, on_device(): lax.all_to_all(best, ('row', 'feat'), 0, 0)  17 us
    pallas_call x1, Pallas kernels, on_device(): pl.pallas_call(gain_kernel, out_shape=(jax.ShapeDtypeStruct((own, NODES),...  13.8 us
    all_to_all x1, waiting for transfers between devices, on_device(): gathered = lax.all_to_all(sent, 'row', 0, 0)  10.3 us
    all_to_all x1, starting transfers between devices, on_device(): gathered = lax.all_to_all(sent, 'row', 0, 0)  7.35 us
    pallas_call x1, Pallas kernels, on_device(): pl.pallas_call(sort_kernel, out_shape=jax.ShapeDtypeStruct((parts, length...  2.74 us
  transfers between devices with their start and end apart: 1, of which 1 were waited for; matrix products, arithmetic and copies ran while one was open for 1% of the time, Pallas kernels for 0%

profile of v2, /device:TPU:1, one launch (start us, length us, event | category | flops | bytes accessed | tf_op | source)
XLA Modules:
  0.0 53.2 jit_solution(2797494422702797023)
XLA Ops:
  0.6 2.7 %sort_rows.1 = bf16[16,152,128]{2,1,0:T(8,128)(2,1)} custom-call(bf16[1024,256]{1,0:T(8,128)(2,1)} %value_in.1, f32[1,1024]{1,0:T(1,128)} %bitcast.10, f32[1,1024]{1,0:T(1,128)} %bitcast.11, s32[1,1024]{1,0:T(1,128)} %bitcast.12), custom_call_target="tpu_custom_call" | custom-call | tf_op jit(solution)/shard_map/sort_rows/pallas_call | solution.py:404
  3.4 7.4 %all-to-all-start = ((bf16[16,152,128]{2,1,0:T(8,128)(2,1)}), bf16[16,152,128]{2,1,0:T(8,128)(2,1)S(1)}, u32[]{:S(2)}, u32[]{:S(2)}) async-start(bf16[16,152,128]{2,1,0:T(8,128)(2,1)} %sort_rows.1), calls=%async_computation | async-start | bytes 1245184 | tf_op jit(solution)/shard_map/all_to_all | solution.py:419
  10.7 0.7 %constant_dynamic-slice_fusion.edge_ref = f32[16,256]{1,0:T(8,128)S(1)} fusion(f32[256,256]{1,0:T(8,128)} %param.6, s32[]{:T(128)S(6)} %select_n.3), kind=kLoop, calls=%fused_computation | loop fusion | bytes 32772 | tf_op jit(solution)/shard_map/dynamic_slice | solution.py:420
  11.5 10.3 %all-to-all-done.sent_ref = bf16[16,152,128]{2,1,0:T(8,128)(2,1)S(1)} async-done(((bf16[16,152,128]{2,1,0:T(8,128)(2,1)}), bf16[16,152,128]{2,1,0:T(8,128)(2,1)S(1)}, u32[]{:S(2)}, u32[]{:S(2)}) %all-to-all-start) | async-done | bytes 622624 | tf_op jit(solution)/shard_map/all_to_all | solution.py:419
  21.8 13.8 %split_gain.1 = (f32[16,32]{1,0:T(8,128)S(1)}, f32[128,32]{1,0:T(8,128)S(1)}) custom-call(bf16[16,152,128]{2,1,0:T(8,128)(2,1)S(1)} %all-to-all-done.sent_ref, f32[16,256]{1,0:T(8,128)S(1)} %constant_dynamic-slice_fusion.edge_ref), custom_call_target="tpu_custom_call" | custom-call | tf_op jit(solution)/shard_map/split_gain/pallas_call | solution.py:422
  35.6 17.0 %all_to_all.16 = f32[128,1,32]{2,1,0:T(1,128)S(1)} all-to-all(f32[128,1,32]{2,1,0:T(1,128)S(1)} %bitcast.9), channel_id=1, replica_groups=mesh['row'=16,'feat'=8] {'row','feat'}, dimensions={0} | all-to-all | bytes 32768 | tf_op jit(solution)/shard_map/all_to_all | solution.py:457
  52.6 0.6 %write_gains.1 = (f32[16,32]{1,0:T(8,128)}, f32[1,32]{1,0:T(1,128)}) custom-call(f32[16,32]{1,0:T(8,128)S(1)} %get-tuple-element.6.own_ref, f32[128,32]{1,0:T(8,128)S(1)} %bitcast.8), custom_call_target="tpu_custom_call" | custom-call | tf_op jit(solution)/shard_map/write_gains/pallas_call | solution.py:447
Async XLA Ops:
  3.4 18.4 %all-to-all-start = ((bf16[16,152,128]{2,1,0:T(8,128)(2,1)}), bf16[16,152,128]{2,1,0:T(8,128)(2,1)S(1)}, u32[]{:S(2)}, u32[]{:S(2)}) async-start(bf16[16,152,128]{2,1,0:T(8,128)(2,1)} %sort_rows.1), calls=%async_computation | async-start | bytes 1245184 | tf_op jit(solution)/shard_map/all_to_all | solution.py:419

commit v3 on v2

--- a/solution.py
+++ b/solution.py
@@ -13,7 +13,7 @@
 PIECE = 32
 QUAD = 4
 NODE_BLOCK = 4
-PAIRED = (0, 2)
+PAIRED = (1, 3)
 
 
 def dot_nt(left, right):

time: 53.2 us -> 53.8 us (1.011)
  no operation moved by 1% of the time
where the time goes in v3:
time: 53.8 us; the launch traced here: 53.5 us
  Pallas kernels  17.5 us (33%)
  blocking collectives  17 us (32%)
  waiting for transfers between devices  10.3 us (19%)
  starting transfers between devices  7.35 us (14%)
  local copies, waits for them, and re-layouts  0.72 us (1%)
  between operations  0.65 us (1%)
    all_to_all x1, blocking collectives, on_device(): lax.all_to_all(best, ('row', 'feat'), 0, 0)  17 us
    pallas_call x1, Pallas kernels, on_device(): pl.pallas_call(gain_kernel, out_shape=(jax.ShapeDtypeStruct((own, NODES),...  14.1 us
    all_to_all x1, waiting for transfers between devices, on_device(): gathered = lax.all_to_all(sent, 'row', 0, 0)  10.3 us
    all_to_all x1, starting transfers between devices, on_device(): gathered = lax.all_to_all(sent, 'row', 0, 0)  7.35 us
    pallas_call x1, Pallas kernels, on_device(): pl.pallas_call(sort_kernel, out_shape=jax.ShapeDtypeStruct((parts, length...  2.74 us
  transfers between devices with their start and end apart: 1, of which 1 were waited for; matrix products, arithmetic and copies ran while one was open for 1% of the time, Pallas kernels for 0%

profile of v3, /device:TPU:1, one launch (start us, length us, event | category | flops | bytes accessed | tf_op | source)
XLA Modules:
  0.0 53.5 jit_solution(13273330739413941240)
XLA Ops:
  0.6 2.7 %sort_rows.1 = bf16[16,152,128]{2,1,0:T(8,128)(2,1)} custom-call(bf16[1024,256]{1,0:T(8,128)(2,1)} %value_in.1, f32[1,1024]{1,0:T(1,128)} %bitcast.10, f32[1,1024]{1,0:T(1,128)} %bitcast.11, s32[1,1024]{1,0:T(1,128)} %bitcast.12), custom_call_target="tpu_custom_call" | custom-call | tf_op jit(solution)/shard_map/sort_rows/pallas_call | solution.py:404
  3.4 7.4 %all-to-all-start = ((bf16[16,152,128]{2,1,0:T(8,128)(2,1)}), bf16[16,152,128]{2,1,0:T(8,128)(2,1)S(1)}, u32[]{:S(2)}, u32[]{:S(2)}) async-start(bf16[16,152,128]{2,1,0:T(8,128)(2,1)} %sort_rows.1), calls=%async_computation | async-start | bytes 1245184 | tf_op jit(solution)/shard_map/all_to_all | solution.py:419
  10.7 0.7 %constant_dynamic-slice_fusion.edge_ref = f32[16,256]{1,0:T(8,128)S(1)} fusion(f32[256,256]{1,0:T(8,128)} %param.6, s32[]{:T(128)S(6)} %select_n.3), kind=kLoop, calls=%fused_computation | loop fusion | bytes 32772 | tf_op jit(solution)/shard_map/dynamic_slice | solution.py:420
  11.5 10.3 %all-to-all-done.sent_ref = bf16[16,152,128]{2,1,0:T(8,128)(2,1)S(1)} async-done(((bf16[16,152,128]{2,1,0:T(8,128)(2,1)}), bf16[16,152,128]{2,1,0:T(8,128)(2,1)S(1)}, u32[]{:S(2)}, u32[]{:S(2)}) %all-to-all-start) | async-done | bytes 622624 | tf_op jit(solution)/shard_map/all_to_all | solution.py:419
  21.8 14.1 %split_gain.1 = (f32[16,32]{1,0:T(8,128)S(1)}, f32[128,32]{1,0:T(8,128)S(1)}) custom-call(bf16[16,152,128]{2,1,0:T(8,128)(2,1)S(1)} %all-to-all-done.sent_ref, f32[16,256]{1,0:T(8,128)S(1)} %constant_dynamic-slice_fusion.edge_ref), custom_call_target="tpu_custom_call" | custom-call | tf_op jit(solution)/shard_map/split_gain/pallas_call | solution.py:422
  35.9 17.0 %all_to_all.16 = f32[128,1,32]{2,1,0:T(1,128)S(1)} all-to-all(f32[128,1,32]{2,1,0:T(1,128)S(1)} %bitcast.9), channel_id=1, replica_groups=mesh['row'=16,'feat'=8] {'row','feat'}, dimensions={0} | all-to-all | bytes 32768 | tf_op jit(solution)/shard_map/all_to_all | solution.py:457
  52.9 0.6 %write_gains.1 = (f32[16,32]{1,0:T(8,128)}, f32[1,32]{1,0:T(1,128)}) custom-call(f32[16,32]{1,0:T(8,128)S(1)} %get-tuple-element.6.own_ref, f32[128,32]{1,0:T(8,128)S(1)} %bitcast.8), custom_call_target="tpu_custom_call" | custom-call | tf_op jit(solution)/shard_map/write_gains/pallas_call | solution.py:447
Async XLA Ops:
  3.4 18.4 %all-to-all-start = ((bf16[16,152,128]{2,1,0:T(8,128)(2,1)}), bf16[16,152,128]{2,1,0:T(8,128)(2,1)S(1)}, u32[]{:S(2)}, u32[]{:S(2)}) async-start(bf16[16,152,128]{2,1,0:T(8,128)(2,1)} %sort_rows.1), calls=%async_computation | async-start | bytes 1245184 | tf_op jit(solution)/shard_map/all_to_all | solution.py:419
